TPU v7x, 128 devices: a whole 4x4x4 slice. The times are simulated.
128 devices in a mesh: dp: 8 (over z, core), tensor: 16 (over x, y).
Axes of the slice: x: 4, y: 4, z: 4, core: 2. Of those that a mesh axis runs over, the one named last changes fastest.
Arguments:
- queries: bfloat16 [4096, 36864], P('dp', 'tensor'), may hold values from -6.8560344 to 6.8560344
- cache: bfloat16 [8, 3072, 576], P('dp', 'tensor'), may hold values from -4 to 4
- offsets: int32 [8], P('dp'), may hold values from 0 to 2560, as said below
- value_up: bfloat16 [64, 512, 128], P('tensor'), may hold values from -0.25 to 0.25
- out_proj: bfloat16 [8192, 3584], P('tensor', 'dp'), may hold values from -0.0625 to 0.0625
- resid: bfloat16 [4096, 3584], P(('dp', 'tensor')), may hold values from -3 to 3
- norm_gain: float32 [3584], replicated, may hold values from 0.25 to 1.75
- routes: int32 [4096, 8], P(('dp', 'tensor')), may hold values from 0 to 127, as said below
- route_weights: float32 [4096, 8], P(('dp', 'tensor')), may hold values from 0.1 to 0.6
- expert_in: bfloat16 [128, 3584, 2048], P(('dp', 'tensor')), may hold values from -0.09375 to 0.09375
- expert_down: bfloat16 [128, 1024, 3584], P(('dp', 'tensor')), may hold values from -0.1875 to 0.1875
Outputs:
- mixed: bfloat16 [4096, 3584], P(('dp', 'tensor'))
Inputs may be any that keep to these rules, and one draw needn't show every extreme that they name: `routes`: each row names 8 different experts. Among the 32 rows of one device (aligned blocks of rows) a quarter of the experts is named 4 times, a quarter 3 times, a quarter once and a quarter never; in every draw one expert is named 4 times in every block. `offsets`: some sequence's offset is 2560; the new tokens' own latents are in the cache at their positions.
All inputs are finite; a program needn't handle non-finite values.
Results may differ from a plain program's by a relative error of at most 0.024.
Values may be sent and summed in bfloat16 or wider, within the bound.
A program may use at most 192 MiB of HBM per device.

v0:
```python
import jax
import jax.numpy as jnp
from jax import lax
from jax.sharding import PartitionSpec as P


def shards(
    queries,
    cache,
    offsets,
    value_up,
    out_proj,
    resid,
    norm_gain,
    routes,
    route_weights,
    expert_in,
    expert_down,
):
    heads_dev = value_up.shape[0]
    latent_width = value_up.shape[1]
    key_width = cache.shape[2]
    tok_grp = queries.shape[0]
    score_scale = (value_up.shape[2] + key_width - latent_width) ** (-0.5)
    query_heads = queries.reshape(tok_grp, heads_dev, key_width)
    start_pos = offsets[0]
    query_pos = start_pos + jnp.arange(tok_grp, dtype=jnp.int32)
    running = jnp.full((heads_dev, tok_grp), -1e30, jnp.float32)
    key_rows = lax.all_gather(cache, "tensor", axis=1, tiled=True)[0]
    key_count = key_rows.shape[0]
    scores = (
        jnp.einsum("thc,kc->htk", query_heads, key_rows, preferred_element_type=jnp.float32)
        * score_scale
    )
    key_pos = jnp.arange(key_count, dtype=jnp.int32)
    visible = key_pos[None, :] <= query_pos[:, None]
    scores = jnp.where(visible[None], scores, jnp.float32(-1e30))
    highest = jnp.maximum(running, jnp.max(scores, axis=2))
    weights = jnp.where(visible[None], jnp.exp(scores - highest[..., None]), jnp.float32(0.0))
    totals = jnp.sum(weights, axis=2)
    weighted = jnp.einsum(
        "htk,kc->htc",
        weights.astype(jnp.bfloat16),
        key_rows[:, :latent_width],
        preferred_element_type=jnp.float32,
    )
    running, totals, weighted = (highest, totals, weighted)
    context = (weighted / totals[..., None]).astype(jnp.bfloat16)
    head_out = jnp.einsum("htc,hcv->thv", context, value_up, preferred_element_type=jnp.float32)
    head_out = head_out.astype(jnp.bfloat16).reshape(tok_grp, -1)
    partial_value = jnp.dot(
        head_out,
        lax.all_gather(out_proj, "dp", axis=1, tiled=True),
        preferred_element_type=jnp.float32,
    )
    tok_dev = resid.shape[0]
    summed_all = lax.psum(partial_value.astype(jnp.bfloat16), "tensor").astype(jnp.float32)
    attn_rows = lax.dynamic_slice_in_dim(summed_all, lax.axis_index("tensor") * tok_dev, tok_dev, 0)
    stream = resid.astype(jnp.float32) + attn_rows
    mean_square = jnp.mean(stream * stream, axis=1, keepdims=True)
    normed = (stream * lax.rsqrt(mean_square + 1e-06) * norm_gain).astype(jnp.bfloat16)
    experts = lax.axis_size("dp") * lax.axis_size("tensor")
    top_count = routes.shape[1]
    capacity = 2 * tok_dev * top_count // experts
    d_model = normed.shape[1]
    hidden_units = expert_down.shape[1]
    flat_ids = routes.reshape(-1)
    onehot = (flat_ids[:, None] == jnp.arange(experts, dtype=jnp.int32)[None, :]).astype(jnp.int32)
    slot_rank = jnp.sum(onehot * (jnp.cumsum(onehot, axis=0) - 1), axis=1)
    slot_index = flat_ids * capacity + slot_rank
    slot_ids = jnp.arange(experts * capacity, dtype=jnp.int32)
    placing = jnp.any(
        slot_ids[:, None, None] == slot_index.reshape(tok_dev, top_count)[None], axis=2
    )
    outgoing = jnp.dot(placing.astype(jnp.bfloat16), normed, preferred_element_type=jnp.float32)
    outgoing = outgoing.astype(jnp.bfloat16).reshape(experts, capacity, d_model)
    row_block = lax.all_to_all(outgoing, ("dp", "tensor"), split_axis=0, concat_axis=0, tiled=True)
    row_shape = row_block.shape
    flat_rows = row_block.reshape(-1, row_shape[-1])
    joint_proj = jnp.dot(flat_rows, expert_in[0], preferred_element_type=jnp.float32)
    hidden = (jax.nn.silu(joint_proj[:, :hidden_units]) * joint_proj[:, hidden_units:]).astype(
        jnp.bfloat16
    )
    expert_out = jnp.dot(hidden, expert_down[0], preferred_element_type=jnp.float32).astype(
        jnp.bfloat16
    )
    returned = lax.all_to_all(
        expert_out.reshape(row_shape), ("dp", "tensor"), split_axis=0, concat_axis=0, tiled=True
    )
    results = returned.reshape(experts * capacity, d_model)
    picked = results[slot_index].reshape(tok_dev, top_count, d_model)
    routed_sum = jnp.einsum("tk,tkd->td", route_weights, picked.astype(jnp.float32))
    return (stream + routed_sum).astype(jnp.bfloat16)


def solution(mesh):
    return jax.shard_map(
        shards,
        mesh=mesh,
        in_specs=(
            P("dp", "tensor"),
            P("dp", "tensor", None),
            P("dp"),
            P("tensor", None, None),
            P("tensor", "dp"),
            P(("dp", "tensor"), None),
            P(),
            P(("dp", "tensor"), None),
            P(("dp", "tensor"), None),
            P(("dp", "tensor"), None, None),
            P(("dp", "tensor"), None, None),
        ),
        out_specs=P(("dp", "tensor"), None),
        check_vma=False,
    )
```

profile of v0, /device:TPU:1, one launch (start us, length us, event | category | flops | bytes accessed | tf_op | source)
XLA Modules:
  0.0 396.2 jit_solution(15991651440541174260)
XLA Ops:
  6.5 0.0 copy-start
  6.5 0.0 all-gather.3.cloned.1.call-start
  6.5 0.7 all-gather.3.cloned.1.call-update
  7.3 0.0 all-gather.5.cloned.1.call-start
  7.3 0.7 all-gather.5.cloned.1.call-update
  8.0 0.0 all-reduce.2.cloned.1.call-start
  8.7 1.3 iota_compare_fusion
  10.0 4.3 %copy.35 = bf16[512,2304]{0,1:T(8,128)(2,1)} copy(bf16[512,2304]{1,0:T(8,128)(2,1)} %param.11) | data formatting | bytes 4718592 | tf_op args[0]
  14.3 48.7 %all-gather.3.cloned.1.call-done = bf16[1,3072,576]{2,1,0:T(8,128)(2,1)} async-done(((bf16[1,192,576]{2,1,0:T(8,128)(2,1)}), bf16[1,3072,576]{2,1,0:T(8,128)(2,1)}) %all-gather.3.cloned.1.call-update) | async-done | bytes 3538960 | tf_op jit(solution)/shard_map/all_gather | solution.py:29
  63.0 18.4 %fusion = (f32[4,512]{1,0:T(4,128)S(1)}, f32[3072,512,4]{1,0,2:T(8,128)}) fusion(pred[512,3072]{0,1:T(8,128)(4,1)S(1)} %iota_compare_fusion, bf16[512,4,576]{0,2,1:T(8,128)(2,1)} %bitcast.61, bf16[1,3072,576]{2,1,0:T(8,128)(2,1)} %all-gather.3.cloned.1.call-done), kind=kOutput, calls=%fused_computation.3 | convolution fusion | flops 7266629632 | bytes 32645120 | tf_op jit(solution)/shard_map/thc,kc->htk/dot_general | solution.py:32
  81.4 6.1 %copy.34 = bf16[1,3072,576]{1,2,0:T(8,128)(2,1)} copy(bf16[1,3072,576]{2,1,0:T(8,128)(2,1)} %all-gather.3.cloned.1.call-done) | data formatting | bytes 7077888 | tf_op jit(solution)/shard_map/all_gather | solution.py:29
  87.5 11.7 %fusion.1 = f32[4,512]{1,0:T(4,128)S(1)} fusion(f32[3072,512,4]{1,0,2:T(8,128)} %get-tuple-element.8, f32[4,512]{1,0:T(4,128)S(1)} %broadcast_maximum_fusion, pred[512,3072]{0,1:T(8,128)(4,1)S(1)} %iota_compare_fusion), kind=kLoop, calls=%fused_computation.4 | loop fusion | flops 31455232 | bytes 26755072 | tf_op jit(solution)/shard_map/reduce_sum | solution.py:40
  99.2 14.4 %fusion.5 = f32[4,512,512]{2,1,0:T(8,128)} fusion(f32[3072,512,4]{1,0,2:T(8,128)} %get-tuple-element.8, f32[4,512]{1,0:T(4,128)S(1)} %broadcast_maximum_fusion, pred[512,3072]{0,1:T(8,128)(4,1)S(1)} %iota_compare_fusion, bf16[3072,576]{0,1:T(8,128)(2,1)} %bitcast.60), kind=kOutput, calls=%fused_computation.8 | convolution fusion | flops 6473908224 | bytes 34086912 | tf_op jit(solution)/shard_map/htk,kc->htc/dot_general | solution.py:41
  113.7 0.0 copy-done
  113.7 3.1 fusion.19
  116.8 0.0 all-gather.5.cloned.1.call-done
  116.8 0.0 copy-start.4
  116.8 6.0 %convolution_convert_fusion.1 = bf16[512,3584]{1,0:T(8,128)(2,1)} fusion(bf16[512,512]{0,1:T(8,128)(2,1)S(1)} %bitcast.65, bf16[512,3584]{0,1:T(8,128)(2,1)} %all-gather.5.cloned.1.call-done), kind=kOutput, calls=%fused_computation.15 | convolution fusion | flops 1880883200 | bytes 7864320 | tf_op jit(solution)/shard_map/dot_general | solution.py:51
  122.8 0.0 all-reduce.2.cloned.1.call-update
  122.8 0.0 copy-done.4
  122.9 0.1 copy.39
  122.9 0.1 eq.43
  123.0 0.1 eq.39
  123.1 0.1 copy.42
  123.2 0.2 fusion.27
  123.5 0.1 add_add_fusion
  123.6 0.2 fusion.28
  123.8 0.1 reduce_sum.33
  123.9 0.2 fusion.22
  124.1 97.0 %all-reduce.2.cloned.1.call-done = bf16[512,3584]{1,0:T(8,128)(2,1)} async-done(((bf16[512,3584]{1,0:T(8,128)(2,1)}), bf16[512,3584]{1,0:T(8,128)(2,1)}) %all-reduce.2.cloned.1.call-update) | async-done | bytes 3670032 | tf_op jit(solution)/shard_map/psum | solution.py:57
  221.1 0.0 copy-done.2
  221.1 1.1 multiply_reduce_fusion
  222.3 4.0 %convolution_convert_fusion = bf16[512,3584]{1,0:T(8,128)(2,1)} fusion(pred[512,32]{0,1:T(8,128)(4,1)S(1)} %fusion.22, bf16[32,3584]{1,0:T(8,128)(2,1)S(1)} %copy-done.2, f32[3584]{0:T(1024)S(1)} %copy-done.3, f32[32]{0:T(128)S(1)} %add_rsqrt_fusion, bf16[512,3584]{1,0:T(8,128)(2,1)} %all-reduce.2.cloned.1.call-done, s32[]{:T(128)S(6)} %select_n.22), kind=kOutput, calls=%fused_computation.14 | convolution fusion | flops 119963648 | bytes 4159620 | tf_op jit(solution)/shard_map/dot_general | solution.py:75
  226.3 7.0 %reshape.114 = bf16[128,4,3584]{2,1,0:T(4,128)(2,1)} reshape(bf16[512,3584]{1,0:T(8,128)(2,1)} %convolution_convert_fusion) | data formatting | bytes 7340032 | tf_op jit(solution)/shard_map/reshape | solution.py:76
  233.3 55.2 %all_to_all.10 = bf16[128,4,3584]{2,1,0:T(4,128)(2,1)} all-to-all(bf16[128,4,3584]{2,1,0:T(4,128)(2,1)} %reshape.114), channel_id=1, replica_groups=mesh['dp'=8,'tensor'=16] {'dp','tensor'}, dimensions={0} | all-to-all | bytes 7340032 | tf_op jit(solution)/shard_map/all_to_all | solution.py:77
  288.5 6.7 %reshape.115 = bf16[512,3584]{1,0:T(8,128)(2,1)} reshape(bf16[128,4,3584]{2,1,0:T(4,128)(2,1)} %all_to_all.10) | data formatting | bytes 7340032 | tf_op jit(solution)/shard_map/reshape | solution.py:79
  295.3 12.1 %fusion.3 = f32[512,2048]{1,0:T(8,128)S(1)} fusion(bf16[512,3584]{1,0:T(8,128)(2,1)} %reshape.115, bf16[1,3584,2048]{2,1,0:T(8,128)(2,1)} %param.20), kind=kOutput, calls=%fused_computation.6 | convolution fusion | flops 7516192768 | bytes 22544384 | tf_op jit(solution)/shard_map/dot_general | solution.py:80
  307.3 8.7 %fusion.10 = bf16[512,3584]{1,0:T(8,128)(2,1)} fusion(bf16[1,1024,3584]{2,1,0:T(8,128)(2,1)} %param.21, f32[512,2048]{1,0:T(8,128)S(1)} %fusion.3), kind=kOutput, calls=%fused_computation.13 | convolution fusion | flops 3763077120 | bytes 15204352 | tf_op jit(solution)/shard_map/dot_general | solution.py:84
  316.0 7.0 %reshape.116 = bf16[128,4,3584]{2,1,0:T(4,128)(2,1)} reshape(bf16[512,3584]{1,0:T(8,128)(2,1)} %fusion.10) | data formatting | bytes 7340032 | tf_op jit(solution)/shard_map/reshape | solution.py:88
  323.0 5.0 %all-to-all-start.1 = ((bf16[128,4,3584]{2,1,0:T(4,128)(2,1)}), bf16[128,4,3584]{2,1,0:T(4,128)(2,1)}, u32[]{:S(2)}, u32[]{:S(2)}) async-start(bf16[128,4,3584]{2,1,0:T(4,128)(2,1)} %reshape.116), calls=%async_computation.1 | async-start | bytes 7340032 | tf_op jit(solution)/shard_map/all_to_all | solution.py:87
  328.1 0.1 mul.73
  328.2 0.1 copy.47
  328.3 46.2 %all-to-all-done.1 = bf16[128,4,3584]{2,1,0:T(4,128)(2,1)} async-done(((bf16[128,4,3584]{2,1,0:T(4,128)(2,1)}), bf16[128,4,3584]{2,1,0:T(4,128)(2,1)}, u32[]{:S(2)}, u32[]{:S(2)}) %all-to-all-start.1) | async-done | bytes 3670048 | tf_op jit(solution)/shard_map/all_to_all | solution.py:87
  374.5 6.7 %reshape.117 = bf16[512,3584]{1,0:T(8,128)(2,1)} reshape(bf16[128,4,3584]{2,1,0:T(4,128)(2,1)} %all-to-all-done.1) | data formatting | bytes 7340032 | tf_op jit(solution)/shard_map/reshape | solution.py:90
  381.3 6.1 %gather_fusion = bf16[256,3584]{1,0:T(8,128)(2,1)S(1)} fusion(bf16[512,3584]{1,0:T(8,128)(2,1)} %reshape.117, s32[1024]{0:T(1024)S(1)} %pad_clamp_fusion), kind=kCustom, calls=%fused_computation | custom fusion | bytes 3671040 | tf_op jit(solution)/shard_map/gather | solution.py:91
  387.4 0.6 fusion.17
  388.0 1.7 fusion.23
  389.7 0.0 copy-done.1
  (16 shorter events, 0.1 us)
Async XLA Ops:
  6.5 107.1 %copy-start = (bf16[4,512,128]{2,1,0:T(8,128)(2,1)S(1)}, bf16[4,512,128]{2,1,0:T(8,128)(2,1)}, u32[]{:S(2)}) copy-start(bf16[4,512,128]{2,1,0:T(8,128)(2,1)} %param.14) | copy-start | bytes 1572868
  6.5 56.5 %all-gather.3.cloned.1.call-start = ((), (), s32[]{:S(2)}) async-start(), calls=%async_computation.2 | async-start | bytes 4177920 | tf_op jit(solution)/shard_map/all_gather | solution.py:29
  7.3 109.5 %all-gather.5.cloned.1.call-start = ((), (), s32[]{:S(2)}) async-start(), calls=%async_computation.3 | async-start | bytes 4128768 | tf_op jit(solution)/shard_map/all_gather | solution.py:53
  8.0 213.1 %all-reduce.2.cloned.1.call-start = ((), (), s32[]{:S(2)}) async-start(), calls=%async_computation.4 | async-start | bytes 7340032 | tf_op jit(solution)/shard_map/psum | solution.py:57
  116.8 6.1 %copy-start.4 = (s32[32,8]{0,1:T(8,128)S(1)}, s32[32,8]{0,1:T(8,128)}, u32[]{:S(2)}) copy-start(s32[32,8]{0,1:T(8,128)} %param.18) | copy-start | bytes 3076
  122.8 98.3 %copy-start.2 = (bf16[32,3584]{1,0:T(8,128)(2,1)S(1)}, bf16[32,3584]{1,0:T(8,128)(2,1)}, u32[]{:S(2)}) copy-start(bf16[32,3584]{1,0:T(8,128)(2,1)} %param.16) | copy-start | bytes 688132
  122.8 99.5 %copy-start.3 = (f32[3584]{0:T(1024)S(1)}, f32[3584]{0:T(1024)}, u32[]{:S(2)}) copy-start(f32[3584]{0:T(1024)} %param.17) | copy-start | bytes 43012
  323.0 5.1 %copy-start.5 = (f32[32,8]{0,1:T(8,128)S(1)}, f32[32,8]{0,1:T(8,128)}, u32[]{:S(2)}) copy-start(f32[32,8]{0,1:T(8,128)} %param.19) | copy-start | bytes 3076
  323.0 51.5 %all-to-all-start.1 = ((bf16[128,4,3584]{2,1,0:T(4,128)(2,1)}), bf16[128,4,3584]{2,1,0:T(4,128)(2,1)}, u32[]{:S(2)}, u32[]{:S(2)}) async-start(bf16[128,4,3584]{2,1,0:T(4,128)(2,1)} %reshape.116), calls=%async_computation.1 | async-start | bytes 7340032 | tf_op jit(solution)/shard_map/all_to_all | solution.py:87
  381.3 8.4 %copy-start.1 = (bf16[4,512,128]{2,1,0:T(8,128)(2,1)S(1)}, bf16[4,512,128]{2,1,0:T(8,128)(2,1)}, u32[]{:S(2)}) copy-start(bf16[4,512,128]{2,1,0:T(8,128)(2,1)} %param.14) | copy-start | bytes 1572868
Sparse Core Ops, SparseCore 0:
  9.5 53.4 all-gather.2
  64.7 30.2 all-gather.4
  123.0 98.1 all-reduce.1
where the time goes:
time: 398 us; the launch traced here: 396 us
  waiting for transfers between devices  193 us (48%)
  matrix products  67.3 us (17%)
  blocking collectives  55.2 us (14%)
  local copies, waits for them, and re-layouts  44.7 us (11%)
  other arithmetic  16.6 us (4%)
  between operations  13.9 us (3%)
  starting transfers between devices  5.11 us (1%)
    psum x1, waiting for transfers between devices, shards(): lax.psum(partial_value.astype(jnp.bfloat16), 'tensor').astype(jnp.float32)  97 us
    all_to_all x1, blocking collectives, shards(): lax.all_to_all(outgoing, ('dp', 'tensor'), split_axis=0, concat_axis=0, t...  55.2 us
    all_gather x1, waiting for transfers between devices, shards(): key_rows = lax.all_gather(cache, 'tensor', axis=1, tiled=True)[0]  48.7 us
    all_to_all x1, waiting for transfers between devices, shards(): lax.all_to_all(expert_out.reshape(row_shape), ('dp', 'tensor'), split_axi...  46.2 us
    dot_general x1, matrix products, shards(): jnp.einsum('thc,kc->htk', query_heads, key_rows, preferred_element_type=j...  18.4 us
    dot_general x1, matrix products, shards(): jnp.einsum('htk,kc->htc', weights.astype(jnp.bfloat16), key_rows[:, :late...  14.4 us
    dot_general x1, matrix products, shards(): jnp.dot(flat_rows, expert_in[0], preferred_element_type=jnp.float32)  12.1 us
    reduce_sum x1, other arithmetic, shards(): totals = jnp.sum(weights, axis=2)  11.7 us
  transfers between devices with their start and end apart: 4, of which 3 were waited for; matrix products, arithmetic and copies ran while one was open for 15% of the time, Pallas kernels for 0%

commit v1 on v0

--- a/solution.py
+++ b/solution.py
@@ -2,6 +2,12 @@
 import jax.numpy as jnp
 from jax import lax
 from jax.sharding import PartitionSpec as P
+
+
+def summed_here(block, axis):
+    parts = lax.all_gather(block, axis, axis=0, tiled=False)
+    total = parts.sum(axis=0)
+    return total
 
 
 def shards(
@@ -54,7 +60,7 @@
         preferred_element_type=jnp.float32,
     )
     tok_dev = resid.shape[0]
-    summed_all = lax.psum(partial_value.astype(jnp.bfloat16), "tensor").astype(jnp.float32)
+    summed_all = summed_here(partial_value.astype(jnp.bfloat16), "tensor").astype(jnp.float32)
     attn_rows = lax.dynamic_slice_in_dim(summed_all, lax.axis_index("tensor") * tok_dev, tok_dev, 0)
     stream = resid.astype(jnp.float32) + attn_rows
     mean_square = jnp.mean(stream * stream, axis=1, keepdims=True)

time: 398 us -> 646 us (1.62)
  waiting for transfers between devices: 193 us -> 421 us
  other arithmetic: 16.6 us -> 38 us
    all_gather x0 -> x1, waiting for transfers between devices: none -> 324 us  [summed_here(): parts = lax.all_gather(block, axis, axis=0, tiled=False)]
    psum x1 -> x0, waiting for transfers between devices: 97 us -> none  [shards(): lax.psum(partial_value.astype(jnp.bfloat16), 'tensor').astype(jnp.float32)]
    reduce_sum x0 -> x1, other arithmetic: none -> 21.4 us  [summed_here(): total = parts.sum(axis=0)]
  transfers between devices with their start and end apart: 4 -> 4, of which waited for: 3 -> 3; matrix products, arithmetic and copies ran while one was open for 15% -> 9% of each run, Pallas kernels for 0% -> 0%
where the time goes in v1:
time: 646 us; the launch traced here: 645 us
  waiting for transfers between devices  421 us (65%)
  matrix products  67.1 us (10%)
  blocking collectives  55.2 us (9%)
  local copies, waits for them, and re-layouts  44.7 us (7%)
  other arithmetic  38 us (6%)
  between operations  13.9 us (2%)
    all_gather x1, waiting for transfers between devices, summed_here(): parts = lax.all_gather(block, axis, axis=0, tiled=False)  324 us
    all_to_all x1, blocking collectives, shards(): lax.all_to_all(outgoing, ('dp', 'tensor'), split_axis=0, concat_axis=0, t...  55.2 us
    all_gather x1, waiting for transfers between devices, shards(): key_rows = lax.all_gather(cache, 'tensor', axis=1, tiled=True)[0]  48.7 us
    all_to_all x1, waiting for transfers between devices, shards(): lax.all_to_all(expert_out.reshape(row_shape), ('dp', 'tensor'), split_axi...  46.5 us
    reduce_sum x1, other arithmetic, summed_here(): total = parts.sum(axis=0)  21.4 us
    dot_general x1, matrix products, shards(): jnp.einsum('thc,kc->htk', query_heads, key_rows, preferred_element_type=j...  18.4 us
    dot_general x1, matrix products, shards(): jnp.einsum('htk,kc->htc', weights.astype(jnp.bfloat16), key_rows[:, :late...  14.4 us
  transfers between devices with their start and end apart: 4, of which 3 were waited for; matrix products, arithmetic and copies ran while one was open for 9% of the time, Pallas kernels for 0%

profile of v1, /device:TPU:1, one launch (start us, length us, event | category | flops | bytes accessed | tf_op | source)
XLA Modules:
  0.0 644.5 jit_solution(16211505197439905512)
XLA Ops:
  6.5 0.0 copy-start
  6.5 0.0 all-gather.5.cloned.1.call-start
  6.5 0.7 all-gather.5.cloned.1.call-update
  7.3 0.0 all-gather.7.cloned.1.call-start
  7.3 0.7 all-gather.7.cloned.1.call-update
  8.0 0.0 all-gather.9.cloned.1.call-start
  8.7 1.3 iota_compare_fusion
  10.0 4.3 copy.35
  14.3 48.7 %all-gather.5.cloned.1.call-done = bf16[1,3072,576]{2,1,0:T(8,128)(2,1)} async-done(((bf16[1,192,576]{2,1,0:T(8,128)(2,1)}), bf16[1,3072,576]{2,1,0:T(8,128)(2,1)}) %all-gather.5.cloned.1.call-update) | async-done | bytes 3538960 | tf_op jit(solution)/shard_map/all_gather | solution.py:35
  63.0 18.4 %fusion = (f32[4,512]{1,0:T(4,128)S(1)}, f32[3072,512,4]{1,0,2:T(8,128)}) fusion(pred[512,3072]{0,1:T(8,128)(4,1)S(1)} %iota_compare_fusion, bf16[512,4,576]{0,2,1:T(8,128)(2,1)} %bitcast.63, bf16[1,3072,576]{2,1,0:T(8,128)(2,1)} %all-gather.5.cloned.1.call-done), kind=kOutput, calls=%fused_computation.3 | convolution fusion | flops 7266629632 | bytes 32645120 | tf_op jit(solution)/shard_map/thc,kc->htk/dot_general | solution.py:38
  81.4 6.1 copy.34
  87.5 11.7 %fusion.1 = f32[4,512]{1,0:T(4,128)S(1)} fusion(f32[3072,512,4]{1,0,2:T(8,128)} %get-tuple-element.8, f32[4,512]{1,0:T(4,128)S(1)} %broadcast_maximum_fusion, pred[512,3072]{0,1:T(8,128)(4,1)S(1)} %iota_compare_fusion), kind=kLoop, calls=%fused_computation.4 | loop fusion | flops 31455232 | bytes 26755072 | tf_op jit(solution)/shard_map/reduce_sum | solution.py:46
  99.2 14.4 %fusion.5 = f32[4,512,512]{2,1,0:T(8,128)} fusion(f32[3072,512,4]{1,0,2:T(8,128)} %get-tuple-element.8, f32[4,512]{1,0:T(4,128)S(1)} %broadcast_maximum_fusion, pred[512,3072]{0,1:T(8,128)(4,1)S(1)} %iota_compare_fusion, bf16[3072,576]{0,1:T(8,128)(2,1)} %bitcast.62), kind=kOutput, calls=%fused_computation.8 | convolution fusion | flops 6473908224 | bytes 34086912 | tf_op jit(solution)/shard_map/htk,kc->htc/dot_general | solution.py:47
  113.7 0.0 copy-done
  113.7 3.1 fusion.19
  116.8 0.0 all-gather.7.cloned.1.call-done
  116.8 0.0 copy-start.4
  116.8 6.0 convolution_convert_fusion.1
  122.8 0.0 all-gather.9.cloned.1.call-update
  122.8 0.0 copy-done.4
  122.8 0.1 copy.39
  122.9 0.1 eq.43
  123.0 0.1 eq.39
  123.1 0.1 copy.42
  123.2 0.2 fusion.27
  123.4 0.1 add_add_fusion
  123.5 0.2 fusion.28
  123.7 0.1 reduce_sum.46
  123.8 0.2 fusion.22
  124.0 324.1 %all-gather.9.cloned.1.call-done = bf16[8192,3584]{1,0:T(8,128)(2,1)} async-done(((bf16[512,3584]{1,0:T(8,128)(2,1)}), bf16[8192,3584]{1,0:T(8,128)(2,1)}) %all-gather.9.cloned.1.call-update) | async-done | bytes 58720272 | tf_op jit(solution)/shard_map/all_gather | solution.py:8
  448.2 21.4 %reduce_sum.44 = bf16[512,3584]{1,0:T(8,128)(2,1)} reduce(bf16[16,512,3584]{2,1,0:T(8,128)(2,1)} %bitcast.61, bf16[]{:T(256)} %constant.19.clone.1), dimensions={0}, to_apply=%region_2.3 | reduce | flops 27525120 | bytes 62390272 | tf_op jit(solution)/shard_map/reduce_sum | solution.py:9
  469.6 0.0 copy-done.2
  469.6 1.1 multiply_reduce_fusion
  470.7 4.0 convolution_convert_fusion
  474.7 7.0 %reshape.114 = bf16[128,4,3584]{2,1,0:T(4,128)(2,1)} reshape(bf16[512,3584]{1,0:T(8,128)(2,1)} %convolution_convert_fusion) | data formatting | bytes 7340032 | tf_op jit(solution)/shard_map/reshape | solution.py:82
  481.7 55.2 %all_to_all.10 = bf16[128,4,3584]{2,1,0:T(4,128)(2,1)} all-to-all(bf16[128,4,3584]{2,1,0:T(4,128)(2,1)} %reshape.114), channel_id=1, replica_groups=mesh['dp'=8,'tensor'=16] {'dp','tensor'}, dimensions={0} | all-to-all | bytes 7340032 | tf_op jit(solution)/shard_map/all_to_all | solution.py:83
  536.9 6.7 %reshape.115 = bf16[512,3584]{1,0:T(8,128)(2,1)} reshape(bf16[128,4,3584]{2,1,0:T(4,128)(2,1)} %all_to_all.10) | data formatting | bytes 7340032 | tf_op jit(solution)/shard_map/reshape | solution.py:85
  543.6 12.1 %fusion.3 = f32[512,2048]{1,0:T(8,128)S(1)} fusion(bf16[512,3584]{1,0:T(8,128)(2,1)} %reshape.115, bf16[1,3584,2048]{2,1,0:T(8,128)(2,1)} %param.20), kind=kOutput, calls=%fused_computation.6 | convolution fusion | flops 7516192768 | bytes 22544384 | tf_op jit(solution)/shard_map/dot_general | solution.py:86
  555.7 8.6 %fusion.10 = bf16[512,3584]{1,0:T(8,128)(2,1)} fusion(bf16[1,1024,3584]{2,1,0:T(8,128)(2,1)} %param.21, f32[512,2048]{1,0:T(8,128)S(1)} %fusion.3), kind=kOutput, calls=%fused_computation.13 | convolution fusion | flops 3763077120 | bytes 15204352 | tf_op jit(solution)/shard_map/dot_general | solution.py:90
  564.3 7.0 %reshape.116 = bf16[128,4,3584]{2,1,0:T(4,128)(2,1)} reshape(bf16[512,3584]{1,0:T(8,128)(2,1)} %fusion.10) | data formatting | bytes 7340032 | tf_op jit(solution)/shard_map/reshape | solution.py:94
  571.3 4.8 all-to-all-start.1
  576.2 0.1 mul.73
  576.3 0.1 copy.47
  576.4 46.5 %all-to-all-done.1 = bf16[128,4,3584]{2,1,0:T(4,128)(2,1)} async-done(((bf16[128,4,3584]{2,1,0:T(4,128)(2,1)}), bf16[128,4,3584]{2,1,0:T(4,128)(2,1)}, u32[]{:S(2)}, u32[]{:S(2)}) %all-to-all-start.1) | async-done | bytes 3670048 | tf_op jit(solution)/shard_map/all_to_all | solution.py:93
  622.8 6.7 %reshape.117 = bf16[512,3584]{1,0:T(8,128)(2,1)} reshape(bf16[128,4,3584]{2,1,0:T(4,128)(2,1)} %all-to-all-done.1) | data formatting | bytes 7340032 | tf_op jit(solution)/shard_map/reshape | solution.py:96
  629.6 6.1 gather_fusion
  635.7 0.6 fusion.17
  636.3 1.7 fusion.23
  (17 shorter events, 0.1 us)
Async XLA Ops:
  6.5 107.1 %copy-start = (bf16[4,512,128]{2,1,0:T(8,128)(2,1)S(1)}, bf16[4,512,128]{2,1,0:T(8,128)(2,1)}, u32[]{:S(2)}) copy-start(bf16[4,512,128]{2,1,0:T(8,128)(2,1)} %param.14) | copy-start | bytes 1572868
  6.5 56.5 %all-gather.5.cloned.1.call-start = ((), (), s32[]{:S(2)}) async-start(), calls=%async_computation.2 | async-start | bytes 4177920 | tf_op jit(solution)/shard_map/all_gather | solution.py:35
  7.3 109.5 %all-gather.7.cloned.1.call-start = ((), (), s32[]{:S(2)}) async-start(), calls=%async_computation.3 | async-start | bytes 4128768 | tf_op jit(solution)/shard_map/all_gather | solution.py:59
  8.0 440.1 %all-gather.9.cloned.1.call-start = ((), (), s32[]{:S(2)}) async-start(), calls=%async_computation.4 | async-start | bytes 62390272 | tf_op jit(solution)/shard_map/all_gather | solution.py:8
  116.8 6.0 copy-start.4
  448.2 21.4 %copy-start.2 = (bf16[32,3584]{1,0:T(8,128)(2,1)S(1)}, bf16[32,3584]{1,0:T(8,128)(2,1)}, u32[]{:S(2)}) copy-start(bf16[32,3584]{1,0:T(8,128)(2,1)} %param.16) | copy-start | bytes 688132
  448.2 22.6 %copy-start.3 = (f32[3584]{0:T(1024)S(1)}, f32[3584]{0:T(1024)}, u32[]{:S(2)}) copy-start(f32[3584]{0:T(1024)} %param.17) | copy-start | bytes 43012
  571.3 4.9 copy-start.5
  571.3 51.5 %all-to-all-start.1 = ((bf16[128,4,3584]{2,1,0:T(4,128)(2,1)}), bf16[128,4,3584]{2,1,0:T(4,128)(2,1)}, u32[]{:S(2)}, u32[]{:S(2)}) async-start(bf16[128,4,3584]{2,1,0:T(4,128)(2,1)} %reshape.116), calls=%async_computation.1 | async-start | bytes 7340032 | tf_op jit(solution)/shard_map/all_to_all | solution.py:93
  629.6 8.4 %copy-start.1 = (bf16[4,512,128]{2,1,0:T(8,128)(2,1)S(1)}, bf16[4,512,128]{2,1,0:T(8,128)(2,1)}, u32[]{:S(2)}) copy-start(bf16[4,512,128]{2,1,0:T(8,128)(2,1)} %param.14) | copy-start | bytes 1572868
Sparse Core Ops, SparseCore 0:
  9.5 53.4 all-gather.4
  64.7 30.2 all-gather.6
  122.9 325.1 all-gather.8
